TPU v7x, 512 devices: a whole 4x4x16 slice. The times are simulated.
512 devices in a mesh: shard: 128 (over y, z, core), tensor: 4 (over x).
Axes of the slice: x: 4, y: 4, z: 16, core: 2. Of those that a mesh axis runs over, the one named last changes fastest.
Arguments:
- expert_grads: bfloat16 [2, 128, 2, 512, 1024], P(None, 'shard', None, None, 'tensor')
- embed_grads: bfloat16 [2, 128, 4096, 512], P(None, 'shard', None, 'tensor')
- small_grads: bfloat16 [2, 128, 512, 36], P(None, 'shard', None, 'tensor')
- expert_master: float32 [2, 512, 1024], P(None, 'shard', 'tensor'), may hold values from -0.2 to 0.2
- expert_first: float32 [2, 512, 1024], P(None, 'shard', 'tensor'), may hold values from -6 to 6
- expert_second: float32 [2, 512, 1024], P(None, 'shard', 'tensor'), may hold values from 0.02 to 0.2
- embed_master: float32 [4096, 512], P('shard', 'tensor'), may hold values from -0.2 to 0.2
- embed_first: float32 [4096, 512], P('shard', 'tensor'), may hold values from -6 to 6
- embed_second: float32 [4096, 512], P('shard', 'tensor'), may hold values from 0.02 to 0.2
- small_master: float32 [512, 36], P('shard', 'tensor'), may hold values from -0.2 to 0.2
- small_first: float32 [512, 36], P('shard', 'tensor'), may hold values from -6 to 6
- small_second: float32 [512, 36], P('shard', 'tensor'), may hold values from 0.02 to 0.2
- class_steps: int32 [4096], P('shard'), may hold values from 1 to 2000
- clip_rms: float32 [], replicated, may hold values from 1 to 1.5
Outputs:
- expert_weights: bfloat16 [2, 512, 1024], P(None, None, 'tensor')
- embed_weights: bfloat16 [4096, 512], P(None, 'tensor')
- small_weights: bfloat16 [512, 36], P(None, 'tensor')
- expert_master_new: float32 [2, 512, 1024], P(None, 'shard', 'tensor')
- expert_first_new: float32 [2, 512, 1024], P(None, 'shard', 'tensor')
- expert_second_new: float32 [2, 512, 1024], P(None, 'shard', 'tensor')
- embed_master_new: float32 [4096, 512], P('shard', 'tensor')
- embed_first_new: float32 [4096, 512], P('shard', 'tensor')
- embed_second_new: float32 [4096, 512], P('shard', 'tensor')
- embed_step: float32 [4096, 512], P('shard', 'tensor')
- small_master_new: float32 [512, 36], P('shard', 'tensor')
- small_first_new: float32 [512, 36], P('shard', 'tensor')
- small_second_new: float32 [512, 36], P('shard', 'tensor')
- clip_scale: float32 [], replicated
All inputs are finite; a program needn't handle non-finite values.
Results may differ from a plain program's by a relative error of at most 0.001.
Values may be sent and summed in bfloat16 or wider, within the bound.
No kernel may reach another device: no remote copies, remote signals or barrier semaphores. Data moves between devices by JAX's collectives and lax.ppermute only.
A program may use at most 64 MiB of HBM per device.

v0:
```python
import jax
import jax.numpy as jnp
from jax import lax
from jax.sharding import PartitionSpec as P

STEP = 1000
P_TOT = 3164160
BETA_ONE = 0.9
BETA_TWO = 0.999
LEARN_RATE = 0.001
DECAY_RATE = 0.1
EPSILON = 1e-08


def local_total(gradients):
    summed = gradients[0, 0].astype(jnp.float32)
    summed = summed + gradients[1, 0].astype(jnp.float32)
    return summed


def finish(first_new, second_new, master, corr_one, corr_two):
    update_step = (
        first_new / corr_one / (jnp.sqrt(second_new / corr_two) + EPSILON) + DECAY_RATE * master
    )
    master_new = master - LEARN_RATE * update_step
    return (master_new, update_step)


def body(
    expert_grads,
    embed_grads,
    small_grads,
    expert_master,
    expert_first,
    expert_second,
    embed_master,
    embed_first,
    embed_second,
    small_master,
    small_first,
    small_second,
    class_steps,
    clip_rms,
):
    expert_local = local_total(expert_grads)
    embed_local = local_total(embed_grads)
    small_local = local_total(small_grads)
    expert_sum = lax.psum_scatter(expert_local, "shard", scatter_dimension=1, tiled=True)
    embed_sum = lax.psum_scatter(embed_local, "shard", scatter_dimension=0, tiled=True)
    small_sum = lax.psum_scatter(small_local, "shard", scatter_dimension=0, tiled=True)
    summed_all = (expert_sum, embed_sum, small_sum)
    squares = (
        jnp.sum(expert_sum * expert_sum)
        + jnp.sum(embed_sum * embed_sum)
        + jnp.sum(small_sum * small_sum)
    )
    total_squares = lax.psum(squares, ("shard", "tensor"))
    clip_factor = clip_rms * jnp.sqrt(P_TOT / total_squares)

    def moments(group_index, first_moment, second_moment):
        scaled = clip_factor * summed_all[group_index]
        return (
            BETA_ONE * first_moment + (1.0 - BETA_ONE) * scaled,
            BETA_TWO * second_moment + (1.0 - BETA_TWO) * scaled * scaled,
        )

    fixed_one = 1.0 - BETA_ONE**STEP
    fixed_two = 1.0 - BETA_TWO**STEP
    row_float = class_steps.astype(jnp.float32)[:, None]
    row_one = 1.0 - BETA_ONE**row_float
    row_two = 1.0 - BETA_TWO**row_float
    expert_first_new, expert_second_new = moments(0, expert_first, expert_second)
    embed_first_new, embed_second_new = moments(1, embed_first, embed_second)
    small_first_new, small_second_new = moments(2, small_first, small_second)
    expert_master_new, expert_update = finish(
        expert_first_new, expert_second_new, expert_master, fixed_one, fixed_two
    )
    embed_master_new, embed_update = finish(
        embed_first_new, embed_second_new, embed_master, row_one, row_two
    )
    small_master_new, small_update = finish(
        small_first_new, small_second_new, small_master, fixed_one, fixed_two
    )
    expert_cast = expert_master_new.astype(jnp.bfloat16)
    embed_cast = embed_master_new.astype(jnp.bfloat16)
    small_cast = small_master_new.astype(jnp.bfloat16)
    expert_weights = lax.all_gather(expert_cast, "shard", axis=1, tiled=True)
    embed_weights = lax.all_gather(embed_cast, "shard", axis=0, tiled=True)
    small_weights = lax.all_gather(small_cast, "shard", axis=0, tiled=True)
    return (
        expert_weights,
        embed_weights,
        small_weights,
        expert_master_new,
        expert_first_new,
        expert_second_new,
        embed_master_new,
        embed_first_new,
        embed_second_new,
        embed_update,
        small_master_new,
        small_first_new,
        small_second_new,
        clip_factor,
    )


def solution(mesh):
    in_specs = (
        P(None, "shard", None, None, "tensor"),
        P(None, "shard", None, "tensor"),
        P(None, "shard", None, "tensor"),
        P(None, "shard", "tensor"),
        P(None, "shard", "tensor"),
        P(None, "shard", "tensor"),
        P("shard", "tensor"),
        P("shard", "tensor"),
        P("shard", "tensor"),
        P("shard", "tensor"),
        P("shard", "tensor"),
        P("shard", "tensor"),
        P("shard"),
        P(),
    )
    out_specs = (
        P(None, None, "tensor"),
        P(None, "tensor"),
        P(None, "tensor"),
        P(None, "shard", "tensor"),
        P(None, "shard", "tensor"),
        P(None, "shard", "tensor"),
        P("shard", "tensor"),
        P("shard", "tensor"),
        P("shard", "tensor"),
        P("shard", "tensor"),
        P("shard", "tensor"),
        P("shard", "tensor"),
        P("shard", "tensor"),
        P(),
    )
    return jax.shard_map(body, mesh=mesh, in_specs=in_specs, out_specs=out_specs, check_vma=False)
```

profile of v0, /device:TPU:1, one launch (start us, length us, event | category | flops | bytes accessed | tf_op | source)
XLA Modules:
  0.0 900.7 jit_solution(16309437702115690155)
XLA Ops:
  7.2 0.0 copy-start
  7.2 0.0 all-reduce.4.cloned.1.call-start
  7.2 2.4 add_bitcast_fusion.1
  9.7 0.0 all-reduce.4.cloned.1.call-update
  9.7 0.0 reduce-scatter.3.cloned.1.call-start
  9.7 0.0 copy-done
  9.7 1.5 add_bitcast_fusion
  11.3 0.0 copy-start.1
  11.3 0.0 copy-start.11
  11.3 0.0 copy-start.2
  11.3 0.0 copy-start.3
  11.3 0.0 copy-start.4
  11.3 0.0 copy-start.5
  11.3 0.0 copy-start.6
  11.3 0.0 copy-start.7
  11.3 0.0 copy-start.8
  11.4 0.0 copy-start.9
  11.4 0.0 copy-start.10
  11.4 0.0 reduce-scatter.3.cloned.1.call-update
  11.4 0.0 all-gather.3.cloned.1.call-start
  11.5 0.5 copy-done.1
  12.1 0.1 copy.38
  12.2 1.3 dynamic-slice
  14.1 498.3 %all-reduce.1 = f32[512,9]{1,0:T(8,128)S(1)} all-reduce(f32[512,9]{1,0:T(8,128)S(1)} %copy.38), channel_id=4, replica_groups=mesh['shard'=128,'tensor'=4] {'shard'}, use_global_device_ids=true, to_apply=%region_4.0.clone | all-reduce | flops 4608 | bytes 36864
  512.4 0.6 multiply_reduce_fusion.2
  513.0 0.0 copy-done.11
  513.0 0.0 all-reduce.4.cloned.1.call-done
  513.1 1.3 multiply_reduce_fusion.1
  514.4 91.1 %reduce-scatter.3.cloned.1.call-done = f32[32,128]{1,0:T(8,128)} async-done(((f32[4096,128]{1,0:T(8,128)}), f32[32,128]{1,0:T(8,128)}) %reduce-scatter.3.cloned.1.call-update) | async-done | bytes 16400 | tf_op jit(solution)/shard_map/reduce_scatter | solution.py:49
  605.5 1.3 multiply_reduce_fusion
  609.4 112.9 %psum.7 = f32[]{:T(128)} all-reduce(f32[]{:T(128)S(6)} %add.84), channel_id=1, replica_groups=mesh['shard'=128,'tensor'=4] {'shard','tensor'}, use_global_device_ids=true, to_apply=%region_6.0 | all-reduce | flops 1 | bytes 8 | tf_op jit(solution)/shard_map/psum | solution.py:57
  723.0 0.0 copy-done.2
  723.0 0.0 copy-done.3
  723.0 0.0 copy-done.4
  723.0 1.4 fusion.4
  724.5 0.0 all-gather.3.cloned.1.call-update
  724.5 0.0 copy-done.5
  724.5 0.0 copy-done.6
  724.5 0.0 copy-done.7
  724.5 1.4 fusion.6
  725.9 81.5 %all_gather.9 = bf16[2,512,256]{2,0,1:T(2,128)(2,1)S(1)} all-gather(bf16[2,4,256]{2,0,1:T(2,128)(2,1)S(1)} %copy.39), channel_id=1, replica_groups=mesh['shard'=128,'tensor'=4] {'shard'}, dimensions={1}, use_global_device_ids=true | all-gather | bytes 528384 | tf_op jit(solution)/shard_map/all_gather | solution.py:87
  807.4 0.9 copy.40
  808.2 0.0 copy-done.8
  808.2 0.0 copy-done.9
  808.2 0.0 copy-done.10
  808.2 0.6 convert_bitcast_fusion
  808.8 81.2 %all-gather = bf16[128,4,9]{2,1,0:T(4,128)(2,1)S(1)} all-gather(bf16[1,4,9]{2,1,0:T(4,128)(2,1)S(1)} %get-tuple-element.56), channel_id=1, replica_groups=mesh['shard'=128,'tensor'=4] {'shard'}, dimensions={0}, use_global_device_ids=true | all-gather | bytes 9288 | tf_op jit(solution)/shard_map/all_gather | solution.py:89
  890.1 0.7 copy.41
  890.8 0.0 all-gather.3.cloned.1.call-done
  890.8 2.3 copy.51
  (4 shorter events, 0.0 us)
Async XLA Ops:
  7.2 2.6 copy-start
  7.2 505.9 %all-reduce.4.cloned.1.call-start = ((), (), s32[]{:S(2)}) async-start(), calls=%async_computation.3 | async-start | bytes 2097152
  9.7 595.8 %reduce-scatter.3.cloned.1.call-start = ((), (), s32[]{:S(2)}) async-start(), calls=%async_computation.1 | async-start | bytes 2113536 | tf_op jit(solution)/shard_map/reduce_scatter | solution.py:49
  11.3 0.7 copy-start.1
  11.3 501.7 %copy-start.11 = (s32[32]{0:T(128)S(1)}, s32[32]{0:T(128)}, u32[]{:S(2)}) copy-start(s32[32]{0:T(128)} %param.26) | copy-start | bytes 388
  11.3 711.7 %copy-start.2 = (f32[32,128]{1,0:T(8,128)S(1)}, f32[32,128]{1,0:T(8,128)}, u32[]{:S(2)}) copy-start(f32[32,128]{1,0:T(8,128)} %param.20) | copy-start | bytes 49156
  11.3 711.7 %copy-start.3 = (f32[32,128]{1,0:T(8,128)S(1)}, f32[32,128]{1,0:T(8,128)}, u32[]{:S(2)}) copy-start(f32[32,128]{1,0:T(8,128)} %param.22) | copy-start | bytes 49156
  11.3 711.7 %copy-start.4 = (f32[32,128]{1,0:T(8,128)S(1)}, f32[32,128]{1,0:T(8,128)}, u32[]{:S(2)}) copy-start(f32[32,128]{1,0:T(8,128)} %param.21) | copy-start | bytes 49156
  11.3 713.2 %copy-start.5 = (f32[2,4,256]{2,1,0:T(4,128)S(1)}, f32[2,4,256]{2,1,0:T(4,128)}, u32[]{:S(2)}) copy-start(f32[2,4,256]{2,1,0:T(4,128)} %param.17) | copy-start | bytes 24580
  11.3 713.2 %copy-start.6 = (f32[2,4,256]{2,1,0:T(4,128)S(1)}, f32[2,4,256]{2,1,0:T(4,128)}, u32[]{:S(2)}) copy-start(f32[2,4,256]{2,1,0:T(4,128)} %param.19) | copy-start | bytes 24580
  11.3 713.2 %copy-start.7 = (f32[2,4,256]{2,1,0:T(4,128)S(1)}, f32[2,4,256]{2,1,0:T(4,128)}, u32[]{:S(2)}) copy-start(f32[2,4,256]{2,1,0:T(4,128)} %param.18) | copy-start | bytes 24580
  11.3 796.9 %copy-start.8 = (f32[4,9]{1,0:T(4,128)S(1)}, f32[4,9]{1,0:T(4,128)}, u32[]{:S(2)}) copy-start(f32[4,9]{1,0:T(4,128)} %param.23) | copy-start | bytes 436
  11.4 796.9 %copy-start.9 = (f32[4,9]{1,0:T(4,128)S(1)}, f32[4,9]{1,0:T(4,128)}, u32[]{:S(2)}) copy-start(f32[4,9]{1,0:T(4,128)} %param.25) | copy-start | bytes 436
  11.4 796.9 %copy-start.10 = (f32[4,9]{1,0:T(4,128)S(1)}, f32[4,9]{1,0:T(4,128)}, u32[]{:S(2)}) copy-start(f32[4,9]{1,0:T(4,128)} %param.24) | copy-start | bytes 436
  11.4 879.4 %all-gather.3.cloned.1.call-start = ((), (), s32[]{:S(2)}) async-start(), calls=%async_computation.2 | async-start | bytes 1056768 | tf_op jit(solution)/shard_map/all_gather | solution.py:88
Sparse Core Ops, SparseCore 0:
  12.1 340.1 all-reduce.3
  357.5 247.9 reduce-scatter.2
  724.6 125.6 all-gather.2
where the time goes:
time: 901 us
  blocking collectives  774 us (86%)
  waiting for transfers between devices  91.2 us (10%)
  between operations  19 us (2%)
  other arithmetic  10.6 us (1%)
    unnamed x1, blocking collectives  498 us
    psum x1, blocking collectives, body(): total_squares = lax.psum(squares, ('shard', 'tensor'))  113 us
    reduce_scatter x1, waiting for transfers between devices, body(): lax.psum_scatter(embed_local, 'shard', scatter_dimension=0, tiled=True)  91.1 us
    all_gather x1, blocking collectives, body(): expert_weights = lax.all_gather(expert_cast, 'shard', axis=1, tiled=True)  81.5 us
    all_gather x1, blocking collectives, body(): small_weights = lax.all_gather(small_cast, 'shard', axis=0, tiled=True)  81.2 us
  transfers between devices with their start and end apart: 3, of which 1 were waited for; matrix products, arithmetic and copies ran while one was open for 1% of the time, Pallas kernels for 0%

commit v1 on v0

--- a/solution.py
+++ b/solution.py
@@ -86,7 +86,9 @@
     small_cast = small_master_new.astype(jnp.bfloat16)
     expert_weights = lax.all_gather(expert_cast, "shard", axis=1, tiled=True)
     embed_weights = lax.all_gather(embed_cast, "shard", axis=0, tiled=True)
-    small_weights = lax.all_gather(small_cast, "shard", axis=0, tiled=True)
+    h_now = jnp.stack([small_cast] * lax.axis_size("shard"))
+    v_now = lax.all_to_all(h_now, "shard", 0, 0)
+    small_weights = jnp.concatenate(v_now, axis=0)
     return (
         expert_weights,
         embed_weights,

time: 901 us -> 861 us (0.956)
  blocking collectives: 774 us -> 696 us
  waiting for transfers between devices: 91.2 us -> 117 us
  starting transfers between devices: 0.12 us -> 11.3 us
    all_gather x1 -> x0, blocking collectives: 81.2 us -> none  [body(): small_weights = lax.all_gather(small_cast, 'shard', axis=0, tiled=True)]
    all_gather x1, waiting for transfers between devices: 0.01 us -> 25.8 us  [body(): embed_weights = lax.all_gather(embed_cast, 'shard', axis=0, tiled=True)]
    all_to_all x0 -> x1, starting transfers between devices: none -> 11.2 us  [body(): v_now = lax.all_to_all(h_now, 'shard', 0, 0)]
  transfers between devices with their start and end apart: 3 -> 4, of which waited for: 1 -> 2; matrix products, arithmetic and copies ran while one was open for 1% -> 1% of each run, Pallas kernels for 0% -> 0%
where the time goes in v1:
time: 861 us
  blocking collectives  696 us (81%)
  waiting for transfers between devices  117 us (14%)
  between operations  19.1 us (2%)
  starting transfers between devices  11.3 us (1%)
  other arithmetic  10.7 us (1%)
    unnamed x1, blocking collectives  498 us
    psum x1, blocking collectives, body(): total_squares = lax.psum(squares, ('shard', 'tensor'))  113 us
    reduce_scatter x1, waiting for transfers between devices, body(): lax.psum_scatter(embed_local, 'shard', scatter_dimension=0, tiled=True)  91.1 us
    all_gather x1, blocking collectives, body(): expert_weights = lax.all_gather(expert_cast, 'shard', axis=1, tiled=True)  84.9 us
    all_gather x1, waiting for transfers between devices, body(): embed_weights = lax.all_gather(embed_cast, 'shard', axis=0, tiled=True)  25.8 us
  transfers between devices with their start and end apart: 4, of which 2 were waited for; matrix products, arithmetic and copies ran while one was open for 1% of the time, Pallas kernels for 0%

profile of v1, /device:TPU:1, one launch (start us, length us, event | category | flops | bytes accessed | tf_op | source)
XLA Modules:
  0.0 860.7 jit_solution(17718128355158944314)
XLA Ops:
  7.2 0.0 copy-start
  7.2 0.0 all-reduce.4.cloned.1.call-start
  7.2 2.4 add_bitcast_fusion.1
  9.7 0.0 all-reduce.4.cloned.1.call-update
  9.7 0.0 reduce-scatter.3.cloned.1.call-start
  9.7 0.0 copy-done
  9.7 1.6 add_bitcast_fusion
  11.3 0.0 copy-start.1
  11.3 0.0 copy-start.11
  11.3 0.0 copy-start.2
  11.3 0.0 copy-start.3
  11.3 0.0 copy-start.4
  11.3 0.0 copy-start.5
  11.3 0.0 copy-start.6
  11.3 0.0 copy-start.7
  11.4 0.0 copy-start.8
  11.4 0.0 copy-start.9
  11.4 0.0 copy-start.10
  11.4 0.0 reduce-scatter.3.cloned.1.call-update
  11.4 0.0 all-gather.2.cloned.1.call-start
  11.5 0.5 copy-done.1
  12.1 0.1 copy.41
  12.2 1.3 dynamic-slice
  14.1 498.2 %all-reduce.1 = f32[512,9]{1,0:T(8,128)S(1)} all-reduce(f32[512,9]{1,0:T(8,128)S(1)} %copy.41), channel_id=4, replica_groups=mesh['shard'=128,'tensor'=4] {'shard'}, use_global_device_ids=true, to_apply=%region_4.0.clone | all-reduce | flops 4608 | bytes 36864
  512.4 0.6 multiply_reduce_fusion.2
  513.0 0.0 copy-done.11
  513.0 0.0 all-reduce.4.cloned.1.call-done
  513.0 1.3 multiply_reduce_fusion.1
  514.4 91.1 %reduce-scatter.3.cloned.1.call-done = f32[32,128]{1,0:T(8,128)} async-done(((f32[4096,128]{1,0:T(8,128)}), f32[32,128]{1,0:T(8,128)}) %reduce-scatter.3.cloned.1.call-update) | async-done | bytes 16400 | tf_op jit(solution)/shard_map/reduce_scatter | solution.py:49
  605.5 1.3 multiply_reduce_fusion
  609.4 112.9 %psum.7 = f32[]{:T(128)} all-reduce(f32[]{:T(128)S(6)} %add.84), channel_id=1, replica_groups=mesh['shard'=128,'tensor'=4] {'shard','tensor'}, use_global_device_ids=true, to_apply=%region_6.0 | all-reduce | flops 1 | bytes 8 | tf_op jit(solution)/shard_map/psum | solution.py:57
  723.0 0.0 copy-done.2
  723.0 0.0 copy-done.3
  723.1 0.0 copy-done.4
  723.1 1.4 fusion.5
  724.5 0.0 all-gather.2.cloned.1.call-update
  724.5 0.0 copy-done.5
  724.5 0.0 copy-done.6
  724.5 0.0 copy-done.7
  724.6 1.4 fusion.7
  725.9 0.0 copy-done.8
  725.9 0.0 copy-done.9
  725.9 0.0 copy-done.10
  725.9 0.6 fusion.3
  726.6 0.7 stack.2
  727.2 11.2 %all-to-all-start = ((bf16[128,4,9]{2,1,0:T(4,128)(2,1)}), bf16[128,4,9]{2,1,0:T(4,128)(2,1)S(1)}, u32[]{:S(2)}, u32[]{:S(2)}) async-start(bf16[128,4,9]{2,1,0:T(4,128)(2,1)} %stack.2), calls=%async_computation.1 | async-start | bytes 262144 | tf_op jit(solution)/shard_map/all_to_all | solution.py:90
  738.5 84.9 %all_gather.6 = bf16[2,512,256]{2,0,1:T(2,128)(2,1)S(1)} all-gather(bf16[2,4,256]{2,0,1:T(2,128)(2,1)S(1)} %copy.42), channel_id=1, replica_groups=mesh['shard'=128,'tensor'=4] {'shard'}, dimensions={1}, use_global_device_ids=true | all-gather | bytes 528384 | tf_op jit(solution)/shard_map/all_gather | solution.py:87
  823.4 0.9 copy.43
  824.3 0.0 all-to-all-done
  824.3 0.7 copy.44
  825.0 25.8 %all-gather.2.cloned.1.call-done = bf16[4096,128]{1,0:T(8,128)(2,1)} async-done(((bf16[32,128]{1,0:T(8,128)(2,1)}), bf16[4096,128]{1,0:T(8,128)(2,1)}) %all-gather.2.cloned.1.call-update) | async-done | bytes 1048592 | tf_op jit(solution)/shard_map/all_gather | solution.py:88
  850.8 2.3 copy.54
  (4 shorter events, 0.0 us)
Async XLA Ops:
  7.2 2.6 copy-start
  7.2 505.8 %all-reduce.4.cloned.1.call-start = ((), (), s32[]{:S(2)}) async-start(), calls=%async_computation.4 | async-start | bytes 2097152
  9.7 595.8 %reduce-scatter.3.cloned.1.call-start = ((), (), s32[]{:S(2)}) async-start(), calls=%async_computation.2 | async-start | bytes 2113536 | tf_op jit(solution)/shard_map/reduce_scatter | solution.py:49
  11.3 0.7 copy-start.1
  11.3 501.7 %copy-start.11 = (s32[32]{0:T(128)S(1)}, s32[32]{0:T(128)}, u32[]{:S(2)}) copy-start(s32[32]{0:T(128)} %param.26) | copy-start | bytes 388
  11.3 711.7 %copy-start.2 = (f32[32,128]{1,0:T(8,128)S(1)}, f32[32,128]{1,0:T(8,128)}, u32[]{:S(2)}) copy-start(f32[32,128]{1,0:T(8,128)} %param.20) | copy-start | bytes 49156
  11.3 711.7 %copy-start.3 = (f32[32,128]{1,0:T(8,128)S(1)}, f32[32,128]{1,0:T(8,128)}, u32[]{:S(2)}) copy-start(f32[32,128]{1,0:T(8,128)} %param.22) | copy-start | bytes 49156
  11.3 711.8 %copy-start.4 = (f32[32,128]{1,0:T(8,128)S(1)}, f32[32,128]{1,0:T(8,128)}, u32[]{:S(2)}) copy-start(f32[32,128]{1,0:T(8,128)} %param.21) | copy-start | bytes 49156
  11.3 713.2 %copy-start.5 = (f32[2,4,256]{2,1,0:T(4,128)S(1)}, f32[2,4,256]{2,1,0:T(4,128)}, u32[]{:S(2)}) copy-start(f32[2,4,256]{2,1,0:T(4,128)} %param.17) | copy-start | bytes 24580
  11.3 713.2 %copy-start.6 = (f32[2,4,256]{2,1,0:T(4,128)S(1)}, f32[2,4,256]{2,1,0:T(4,128)}, u32[]{:S(2)}) copy-start(f32[2,4,256]{2,1,0:T(4,128)} %param.19) | copy-start | bytes 24580
  11.3 713.2 %copy-start.7 = (f32[2,4,256]{2,1,0:T(4,128)S(1)}, f32[2,4,256]{2,1,0:T(4,128)}, u32[]{:S(2)}) copy-start(f32[2,4,256]{2,1,0:T(4,128)} %param.18) | copy-start | bytes 24580
  11.4 714.6 %copy-start.8 = (f32[4,9]{1,0:T(4,128)S(1)}, f32[4,9]{1,0:T(4,128)}, u32[]{:S(2)}) copy-start(f32[4,9]{1,0:T(4,128)} %param.23) | copy-start | bytes 436
  11.4 714.6 %copy-start.9 = (f32[4,9]{1,0:T(4,128)S(1)}, f32[4,9]{1,0:T(4,128)}, u32[]{:S(2)}) copy-start(f32[4,9]{1,0:T(4,128)} %param.25) | copy-start | bytes 436
  11.4 714.6 %copy-start.10 = (f32[4,9]{1,0:T(4,128)S(1)}, f32[4,9]{1,0:T(4,128)}, u32[]{:S(2)}) copy-start(f32[4,9]{1,0:T(4,128)} %param.24) | copy-start | bytes 436
  11.4 839.3 %all-gather.2.cloned.1.call-start = ((), (), s32[]{:S(2)}) async-start(), calls=%async_computation.3 | async-start | bytes 1056768 | tf_op jit(solution)/shard_map/all_gather | solution.py:88
  727.2 97.0 %all-to-all-start = ((bf16[128,4,9]{2,1,0:T(4,128)(2,1)}), bf16[128,4,9]{2,1,0:T(4,128)(2,1)S(1)}, u32[]{:S(2)}, u32[]{:S(2)}) async-start(bf16[128,4,9]{2,1,0:T(4,128)(2,1)} %stack.2), calls=%async_computation.1 | async-start | bytes 262144 | tf_op jit(solution)/shard_map/all_to_all | solution.py:90
Sparse Core Ops, SparseCore 0:
  12.1 340.0 all-reduce.3
  357.5 247.9 reduce-scatter.2
  724.6 126.0 all-gather.1
